TPU v7x, 32 devices: a whole 2x2x4 slice. The times are simulated.
32 devices in a mesh: mp: 8 (over z, y), dp: 4 (over x, core).
Axes of the slice: x: 2, y: 2, z: 4, core: 2. Of those that a mesh axis runs over, the one named last changes fastest.
Arguments:
- forward_fields: bfloat16 [16, 4, 16384], P(None, None, 'mp'), may hold values from -6 to 6
- adjoint_fields: bfloat16 [64, 4, 16384], P(None, None, 'mp'), may hold values from -6 to 6
- data_rec: int32 [768], P('dp'), may hold values from 0 to 63
- data_freq: int32 [768], P('dp'), may hold values from 0 to 15
- data_coef: float32 [768, 4], P('dp'), may hold values from -6 to 6
- residual_cols: bfloat16 [768, 256], P('dp'), may hold values from -6 to 6
Outputs:
- data_update: bfloat16 [768, 256], P('dp')
- model_update: float32 [16384, 256], P(('mp', 'dp'))
All inputs are finite; a program needn't handle non-finite values.
Results may differ from a plain program's by a relative error of at most 0.0075.
Values may be sent and summed in bfloat16 or wider, within the bound.
A program may use at most 64 MiB of HBM per device.

v0:
```python
import math
import jax
import jax.numpy as jnp
from jax import lax
from jax.sharding import PartitionSpec as P

GRID_COLS = 128
SWEEPS = 2


def with_halo(array, sides, width):
    for axis, dim in sides:
        peers, length = (lax.axis_size(axis), array.shape[dim])
        up = [(i, (i + 1) % peers) for i in range(peers - 1)]
        down = [(j, i) for i, j in up]
        last = lax.slice_in_dim(array, length - width, length, axis=dim)
        leading = lax.slice_in_dim(array, 0, width, axis=dim)
        before = lax.ppermute(last, axis, up)
        after = lax.ppermute(leading, axis, down)
        array = jnp.concatenate([before, array, after], axis=dim)
    return array


def sweep_once(field):
    center = field[:, 1:-1, :]
    sides = jnp.pad(center, ((0, 0), (0, 0), (1, 1)))
    beside_all = field[:, :-2, :] + field[:, 2:, :] + sides[:, :, :-2] + sides[:, :, 2:]
    return center + 0.2 * (beside_all - 4.0 * center)


def per_device(forward_fields, adjoint_fields, data_rec, data_freq, data_coef, residual_cols):
    rows_here = data_rec.shape[0]
    cells_here = forward_fields.shape[2]
    slab_rows = cells_here // GRID_COLS
    slab_count = lax.axis_size("mp")
    block_count = lax.axis_size("dp")
    adjoint = adjoint_fields[data_rec].astype(jnp.float32)
    forward = forward_fields[data_freq].astype(jnp.float32)
    sens = (0.5 * jnp.sum(data_coef[:, :, None] * adjoint * forward, axis=1)).astype(jnp.bfloat16)
    grid = sens.astype(jnp.float32).reshape(rows_here, slab_rows, GRID_COLS)
    extended = with_halo(grid.astype(jnp.bfloat16), (("mp", 1),), SWEEPS).astype(grid.dtype)
    first_row = lax.axis_index("mp") * slab_rows
    total_rows = slab_rows * slab_count
    for sweep in range(SWEEPS):
        extended = sweep_once(extended)
        margin = SWEEPS - 1 - sweep
        if margin > 0:
            global_rows = first_row - margin + jnp.arange(slab_rows + 2 * margin, dtype=jnp.int32)
            inside = (global_rows >= 0) & (global_rows < total_rows)
            extended = jnp.where(inside[None, :, None], extended, 0.0)
    grid = extended
    smooth = grid.reshape(rows_here, cells_here).astype(jnp.bfloat16)
    residual_whole = lax.all_gather(residual_cols, "dp", axis=0, tiled=True)
    gram_tile = lax.dot_general(
        smooth,
        lax.all_gather(sens, "dp", axis=0, tiled=True),
        (((1,), (1,)), ((), ())),
        preferred_element_type=jnp.float32,
    )
    partial_value = jnp.dot(
        gram_tile, residual_whole.astype(jnp.float32), precision=lax.Precision.HIGHEST
    )
    gram_prod = lax.psum(partial_value, "mp") / (cells_here * slab_count)
    data_update = (gram_prod + residual_cols.astype(jnp.float32)).astype(jnp.bfloat16)
    summed = lax.psum_scatter(
        lax.dot_general(
            smooth, data_update, (((0,), (0,)), ((), ())), preferred_element_type=jnp.float32
        ),
        "dp",
        scatter_dimension=0,
        tiled=True,
    )
    model_update = summed / math.sqrt(rows_here * block_count)
    return (data_update, model_update)


def solution(mesh):
    in_specs = (
        P(None, None, "mp"),
        P(None, None, "mp"),
        P("dp"),
        P("dp"),
        P("dp", None),
        P("dp", None),
    )
    out_specs = (P("dp", None), P(("mp", "dp"), None))
    return jax.shard_map(
        per_device, mesh=mesh, in_specs=in_specs, out_specs=out_specs, check_vma=False
    )
```

profile of v0, /device:TPU:0, one launch (start us, length us, event | category | flops | bytes accessed | tf_op | source)
XLA Modules:
  0.0 189.3 jit_solution(5085543405692865950)
XLA Ops:
  7.2 0.0 copy-start
  7.2 0.0 all-gather.2.cloned.1.call-start
  7.2 0.8 compare_select_fusion.1
  8.0 0.7 compare_select_fusion
  8.7 0.8 copy.10
  9.5 0.0 copy-done
  9.5 0.0 copy-start.1
  9.5 9.6 %gather_fusion = bf16[192,4,2048]{2,1,0:T(4,128)(2,1)} fusion(bf16[64,4,2048]{2,1,0:T(4,128)(2,1)S(1)} %copy-done, s32[1024]{0:T(1024)S(1)} %pad_clamp_fusion.1), kind=kCustom, calls=%fused_computation | custom fusion | bytes 6292224 | tf_op jit(solution)/shard_map/gather | solution.py:37
  19.1 0.0 copy-done.1
  19.1 9.7 %gather_fusion.1 = bf16[192,4,2048]{2,1,0:T(4,128)(2,1)} fusion(bf16[16,4,2048]{2,1,0:T(4,128)(2,1)S(1)} %copy-done.1, s32[1024]{0:T(1024)S(1)} %pad_clamp_fusion), kind=kCustom, calls=%fused_computation.1 | custom fusion | bytes 6292224 | tf_op jit(solution)/shard_map/gather | solution.py:38
  28.8 9.7 %multiply_reduce_fusion = f32[192,2048]{1,0:T(8,128)S(1)} fusion(bf16[192,4,2048]{2,1,0:T(4,128)(2,1)} %gather_fusion.1, bf16[192,4,2048]{2,1,0:T(4,128)(2,1)} %gather_fusion, f32[192,4]{1,0:T(8,128)S(1)} %copy.10), kind=kLoop, calls=%fused_computation.2 | loop fusion | flops 7471104 | bytes 7867392 | tf_op jit(solution)/shard_map/reduce_sum | solution.py:39
  38.5 0.0 copy-start.3
  38.5 1.0 multiply_convert_fusion
  39.5 0.0 all-gather.2.cloned.1.call-update
  39.5 0.0 all-reduce.4.cloned.1.call-start
  39.6 1.4 copy.14
  41.0 4.9 %collective-permute-start = (bf16[192,2,128]{0,2,1:T(8,128)(2,1)S(1)}, bf16[192,2,128]{0,2,1:T(8,128)(2,1)S(1)}, u32[]{:S(2)}, u32[]{:S(2)}) collective-permute-start(bf16[192,2,128]{0,2,1:T(8,128)(2,1)S(1)} %get-tuple-element.2), channel_id=1, source_target_pairs={{0,4},{4,8},{8,12},{12,16},{16,20},{20,24},{24,28},{1,5},{5,9},{9,... | collective-permute-start | bytes 294920 | tf_op jit(solution)/shard_map/ppermute | solution.py:18
  46.0 1.3 collective-permute-start.1
  47.3 0.0 copy-done.3
  47.3 7.1 %all_gather.7 = bf16[768,256]{1,0:T(8,128)(2,1)S(1)} all-gather(bf16[192,256]{1,0:T(8,128)(2,1)S(1)} %copy-done.3), channel_id=1, replica_groups=mesh['mp'=8,'dp'=4] {'dp'}, dimensions={0}, use_global_device_ids=true | all-gather | bytes 491520 | tf_op jit(solution)/shard_map/all_gather | solution.py:53
  54.4 0.0 collective-permute-done
  54.4 0.0 collective-permute-done.1
  54.4 0.3 maximum_convert_fusion
  54.7 0.2 slice.54
  54.9 1.0 fusion.5
  55.9 0.1 slice.57
  56.1 0.8 fusion.11
  56.9 14.4 %all-gather.2.cloned.1.call-done = bf16[768,2048]{1,0:T(8,128)(2,1)} async-done(((bf16[192,2048]{1,0:T(8,128)(2,1)}), bf16[768,2048]{1,0:T(8,128)(2,1)}) %all-gather.2.cloned.1.call-update) | async-done | bytes 3145744 | tf_op jit(solution)/shard_map/all_gather | solution.py:56
  71.3 3.1 %fusion.13 = f32[192,768]{1,0:T(8,128)S(1)} fusion(bf16[192,2048]{0,1:T(8,128)(2,1)S(1)} %bitcast.10, bf16[768,2048]{1,0:T(8,128)(2,1)} %all-gather.2.cloned.1.call-done), kind=kOutput, calls=%fused_computation.31 | convolution fusion | flops 603979776 | bytes 4521984 | tf_op jit(solution)/shard_map/dot_general | solution.py:54
  74.4 1.1 fusion.14
  75.5 0.0 all-reduce.4.cloned.1.call-update
  75.5 0.0 reduce-scatter.2.cloned.1.call-start
  75.6 72.2 %all-reduce.4.cloned.1.call-done = f32[192,256]{1,0:T(8,128)} async-done(((f32[192,256]{1,0:T(8,128)}), f32[192,256]{1,0:T(8,128)}) %all-reduce.4.cloned.1.call-update) | async-done | bytes 196624 | tf_op jit(solution)/shard_map/psum | solution.py:63
  147.8 1.0 add_convert_fusion
  148.7 0.0 copy-start.2
  148.7 1.8 fusion.15
  150.5 0.0 reduce-scatter.2.cloned.1.call-update
  150.5 0.0 copy-done.2
  150.5 30.3 %reduce-scatter.2.cloned.1.call-done = f32[512,256]{1,0:T(8,128)} async-done(((f32[2048,256]{1,0:T(8,128)}), f32[512,256]{1,0:T(8,128)}) %reduce-scatter.2.cloned.1.call-update) | async-done | bytes 524304 | tf_op jit(solution)/shard_map/reduce_scatter | solution.py:65
  180.9 1.9 broadcast_multiply_fusion
  (4 shorter events, 0.0 us)
Async XLA Ops:
  7.2 2.3 %copy-start = (bf16[64,4,2048]{2,1,0:T(4,128)(2,1)S(1)}, bf16[64,4,2048]{2,1,0:T(4,128)(2,1)}, u32[]{:S(2)}) copy-start(bf16[64,4,2048]{2,1,0:T(4,128)(2,1)} %param.7) | copy-start | bytes 3145732
  7.2 64.1 %all-gather.2.cloned.1.call-start = ((), (), s32[]{:S(2)}) async-start(), calls=%async_computation.1 | async-start | bytes 3932160 | tf_op jit(solution)/shard_map/all_gather | solution.py:56
  9.5 9.6 %copy-start.1 = (bf16[16,4,2048]{2,1,0:T(4,128)(2,1)S(1)}, bf16[16,4,2048]{2,1,0:T(4,128)(2,1)}, u32[]{:S(2)}) copy-start(bf16[16,4,2048]{2,1,0:T(4,128)(2,1)} %param.6) | copy-start | bytes 786436
  38.5 8.8 %copy-start.3 = (bf16[192,256]{1,0:T(8,128)(2,1)S(1)}, bf16[192,256]{1,0:T(8,128)(2,1)}, u32[]{:S(2)}) copy-start(bf16[192,256]{1,0:T(8,128)(2,1)} %param.11) | copy-start | bytes 294916
  39.5 108.3 %all-reduce.4.cloned.1.call-start = ((), (), s32[]{:S(2)}) async-start(), calls=%async_computation.2 | async-start | bytes 393216 | tf_op jit(solution)/shard_map/psum | solution.py:63
  41.0 13.3 %collective-permute-start = (bf16[192,2,128]{0,2,1:T(8,128)(2,1)S(1)}, bf16[192,2,128]{0,2,1:T(8,128)(2,1)S(1)}, u32[]{:S(2)}, u32[]{:S(2)}) collective-permute-start(bf16[192,2,128]{0,2,1:T(8,128)(2,1)S(1)} %get-tuple-element.2), channel_id=1, source_target_pairs={{0,4},{4,8},{8,12},{12,16},{16,20},{20,24},{24,28},{1,5},{5,9},{9,... | collective-permute-start | bytes 294920 | tf_op jit(solution)/shard_map/ppermute | solution.py:18
  46.0 8.4 %collective-permute-start.1 = (bf16[192,2,128]{0,2,1:T(8,128)(2,1)S(1)}, bf16[192,2,128]{0,2,1:T(8,128)(2,1)S(1)}, u32[]{:S(2)}, u32[]{:S(2)}) collective-permute-start(bf16[192,2,128]{0,2,1:T(8,128)(2,1)S(1)} %get-tuple-element.3), channel_id=1, source_target_pairs={{4,0},{8,4},{12,8},{16,12},{20,16},{24,20},{28,24},{5,1},{9,5},{13... | collective-permute-start | bytes 294920 | tf_op jit(solution)/shard_map/ppermute | solution.py:19
  75.5 105.4 %reduce-scatter.2.cloned.1.call-start = ((), (), s32[]{:S(2)}) async-start(), calls=%async_computation.3 | async-start | bytes 2621440 | tf_op jit(solution)/shard_map/reduce_scatter | solution.py:65
  148.7 1.8 copy-start.2
Sparse Core Ops, SparseCore 0:
  39.6 31.6 all-gather.1
  75.7 72.0 all-reduce.3
  150.7 30.1 reduce-scatter.1
where the time goes:
time: 190 us; the launch traced here: 189 us
  waiting for transfers between devices  117 us (62%)
  local copies, waits for them, and re-layouts  21.9 us (12%)
  other arithmetic  17.1 us (9%)
  between operations  13.9 us (7%)
  blocking collectives  7.1 us (4%)
  starting transfers between devices  6.32 us (3%)
  matrix products  5.98 us (3%)
    psum x1, waiting for transfers between devices, per_device(): gram_prod = lax.psum(partial_value, 'mp') / (cells_here * slab_count)  72.2 us
    reduce_scatter x1, waiting for transfers between devices, per_device(): lax.psum_scatter(lax.dot_general(smooth, data_update, (((0,), (0,)), ((),...  30.3 us
    all_gather x1, waiting for transfers between devices, per_device(): lax.all_gather(sens, 'dp', axis=0, tiled=True)  14.4 us
    gather x1, local copies, waits for them, and re-layouts, per_device(): forward = forward_fields[data_freq].astype(jnp.float32)  9.69 us
    reduce_sum x1, other arithmetic, per_device(): jnp.sum(data_coef[:, :, None] * adjoint * forward, axis=1)  9.66 us
    gather x1, local copies, waits for them, and re-layouts, per_device(): adjoint = adjoint_fields[data_rec].astype(jnp.float32)  9.62 us
    all_gather x1, blocking collectives, per_device(): residual_whole = lax.all_gather(residual_cols, 'dp', axis=0, tiled=True)  7.1 us
    ppermute x1, starting transfers between devices, with_halo(): before = lax.ppermute(last, axis, up)  4.91 us
  transfers between devices with their start and end apart: 5, of which 3 were waited for; matrix products, arithmetic and copies ran while one was open for 2% of the time, Pallas kernels for 0%

commit v1 on v0

--- a/solution.py
+++ b/solution.py
@@ -6,6 +6,27 @@
 
 GRID_COLS = 128
 SWEEPS = 2
+
+
+def push_block(load, array_dim):
+    load = jnp.moveaxis(load, 0, array_dim)
+    t1 = load.shape
+    return load.reshape(*t1[:array_dim], t1[array_dim] * t1[array_dim + 1], *t1[array_dim + 2 :])
+
+
+def match_modes_in(sheet, axis_id):
+    value_now = sheet[None]
+    n = lax.axis_size(axis_id)
+    for tick in range(n.bit_length() - 1):
+        part_now = 1 << tick
+        res = lax.ppermute(
+            value_now, axis_id, list(map(lambda dev_j: (dev_j, dev_j ^ part_now), range(n)))
+        )
+        low = jnp.stack([value_now, res], axis=0)
+        block_now = lax.axis_index(axis_id)
+        long_array = block_now >> tick & 1
+        value_now = jnp.where(long_array == 0, low, low[::-1]).reshape(-1, *sheet.shape)
+    return value_now
 
 
 def with_halo(array, sides, width):
@@ -51,9 +72,14 @@
     grid = extended
     smooth = grid.reshape(rows_here, cells_here).astype(jnp.bfloat16)
     residual_whole = lax.all_gather(residual_cols, "dp", axis=0, tiled=True)
+
+    def draw_tiles(w_in, sample, at_axis):
+        w2 = match_modes_in(w_in, sample)
+        return push_block(w2, at_axis)
+
     gram_tile = lax.dot_general(
         smooth,
-        lax.all_gather(sens, "dp", axis=0, tiled=True),
+        draw_tiles(sens, "dp", at_axis=0),
         (((1,), (1,)), ((), ())),
         preferred_element_type=jnp.float32,
     )

time: 190 us -> 208 us (1.095)
  blocking collectives: 7.1 us -> 32.4 us
  waiting for transfers between devices: 117 us -> 105 us
  other arithmetic: 17.1 us -> 22.2 us
    all_gather x1, blocking collectives: 7.1 us -> 32.4 us  [per_device(): residual_whole = lax.all_gather(residual_cols, 'dp', axis=0, tiled=True)]
    all_gather x1 -> x0, waiting for transfers between devices: 14.4 us -> none  [per_device(): lax.all_gather(sens, 'dp', axis=0, tiled=True)]
    another operation x0 -> x3, other arithmetic: none -> 3.99 us  [match_modes_in(): low = jnp.stack([value_now, res], axis=0)]
    ppermute x0 -> x2, starting transfers between devices: none -> 3.33 us  [match_modes_in(): lax.ppermute(value_now, axis_id, list(map(lambda dev_j: (dev_j, dev_j ^ p...]
  transfers between devices with their start and end apart: 5 -> 6, of which waited for: 3 -> 3; matrix products, arithmetic and copies ran while one was open for 2% -> 2% of each run, Pallas kernels for 0% -> 0%
where the time goes in v1:
time: 208 us; the launch traced here: 207 us
  waiting for transfers between devices  105 us (50%)
  blocking collectives  32.4 us (16%)
  other arithmetic  22.2 us (11%)
  local copies, waits for them, and re-layouts  21.6 us (10%)
  between operations  14.2 us (7%)
  starting transfers between devices  8.14 us (4%)
  matrix products  4.09 us (2%)
    psum x1, waiting for transfers between devices, per_device(): gram_prod = lax.psum(partial_value, 'mp') / (cells_here * slab_count)  72.2 us
    all_gather x1, blocking collectives, per_device(): residual_whole = lax.all_gather(residual_cols, 'dp', axis=0, tiled=True)  32.4 us
    reduce_scatter x1, waiting for transfers between devices, per_device(): lax.psum_scatter(lax.dot_general(smooth, data_update, (((0,), (0,)), ((),...  30.3 us
    gather x1, local copies, waits for them, and re-layouts, per_device(): forward = forward_fields[data_freq].astype(jnp.float32)  9.69 us
    gather x1, local copies, waits for them, and re-layouts, per_device(): adjoint = adjoint_fields[data_rec].astype(jnp.float32)  9.61 us
    reduce_sum x1, other arithmetic, per_device(): jnp.sum(data_coef[:, :, None] * adjoint * forward, axis=1)  9.57 us
  transfers between devices with their start and end apart: 6, of which 3 were waited for; matrix products, arithmetic and copies ran while one was open for 2% of the time, Pallas kernels for 0%

profile of v1, /device:TPU:0, one launch (start us, length us, event | category | flops | bytes accessed | tf_op | source)
XLA Modules:
  0.0 207.3 jit_solution(18251442818615826535)
XLA Ops:
  7.2 0.0 copy-start
  7.2 0.0 all-reduce.4.cloned.1.call-start
  7.2 0.8 compare_select_fusion.1
  8.0 0.7 compare_select_fusion
  8.7 0.8 copy.10
  9.5 0.0 copy-done
  9.5 0.0 copy-start.1
  9.5 9.6 %gather_fusion = bf16[192,4,2048]{2,1,0:T(4,128)(2,1)} fusion(bf16[64,4,2048]{2,1,0:T(4,128)(2,1)S(1)} %copy-done, s32[1024]{0:T(1024)S(1)} %pad_clamp_fusion.1), kind=kCustom, calls=%fused_computation | custom fusion | bytes 6292224 | tf_op jit(solution)/shard_map/gather | solution.py:58
  19.1 0.0 copy-done.1
  19.1 9.7 %gather_fusion.1 = bf16[192,4,2048]{2,1,0:T(4,128)(2,1)} fusion(bf16[16,4,2048]{2,1,0:T(4,128)(2,1)S(1)} %copy-done.1, s32[1024]{0:T(1024)S(1)} %pad_clamp_fusion), kind=kCustom, calls=%fused_computation.1 | custom fusion | bytes 6292224 | tf_op jit(solution)/shard_map/gather | solution.py:59
  28.8 9.6 %multiply_reduce_fusion = f32[192,2048]{1,0:T(8,128)S(1)} fusion(bf16[192,4,2048]{2,1,0:T(4,128)(2,1)} %gather_fusion.1, bf16[192,4,2048]{2,1,0:T(4,128)(2,1)} %gather_fusion, f32[192,4]{1,0:T(8,128)S(1)} %copy.10), kind=kLoop, calls=%fused_computation.2 | loop fusion | flops 7471104 | bytes 7867392 | tf_op jit(solution)/shard_map/reduce_sum | solution.py:60
  38.4 1.0 fusion.25
  39.4 0.5 collective-permute-start.2
  39.9 0.1 fusion.24
  40.0 2.0 collective-permute-done.2
  42.0 0.1 pad_maximum_fusion.1
  42.2 2.2 %fusion.13 = (bf16[1,2,192,2048]{3,2,1,0:T(8,128)(2,1)}, bf16[2,192,2048]{2,1,0:T(8,128)(2,1)}) fusion(bf16[2,1,192,2048]{3,2,0,1:T(8,128)(2,1)S(1)} %pad_maximum_fusion.1, pred[]{:T(512)S(6)} %eq.7), kind=kLoop, calls=%fused_computation.28 | loop fusion | flops 786432 | bytes 4718593 | tf_op jit(solution)/shard_map/stack;reshape | solution.py:25
  44.3 0.0 copy-start.4
  44.3 2.9 %collective-permute-start.3 = (bf16[2,192,2048]{2,1,0:T(8,128)(2,1)}, bf16[2,192,2048]{2,1,0:T(8,128)(2,1)}, u32[]{:S(2)}, u32[]{:S(2)}) collective-permute-start(bf16[2,192,2048]{2,1,0:T(8,128)(2,1)} %get-tuple-element.3), channel_id=1, source_target_pairs={{0,2},{1,3},{2,0},{3,1},{4,6},{5,7},{6,4},{7,5},{8,10},{9,11},{10,... | collective-permute-start | bytes 4718600 | tf_op jit(solution)/shard_map/ppermute | solution.py:22
  47.2 0.1 multiply_convert_fusion
  47.3 0.5 copy.15
  47.8 3.4 %collective-permute-start = (bf16[192,2,128]{0,2,1:T(8,128)(2,1)S(1)}, bf16[192,2,128]{0,2,1:T(8,128)(2,1)S(1)}, u32[]{:S(2)}, u32[]{:S(2)}) collective-permute-start(bf16[192,2,128]{0,2,1:T(8,128)(2,1)S(1)} %get-tuple-element.4), channel_id=1, source_target_pairs={{0,4},{4,8},{8,12},{12,16},{16,20},{20,24},{24,28},{1,5},{5,9},{9,... | collective-permute-start | bytes 294920 | tf_op jit(solution)/shard_map/ppermute | solution.py:39
  51.3 1.3 collective-permute-start.1
  52.6 0.0 copy-done.4
  52.6 32.4 %all_gather.3 = bf16[768,256]{1,0:T(8,128)(2,1)S(1)} all-gather(bf16[192,256]{1,0:T(8,128)(2,1)S(1)} %copy-done.4), channel_id=1, replica_groups=mesh['mp'=8,'dp'=4] {'dp'}, dimensions={0}, use_global_device_ids=true | all-gather | bytes 491520 | tf_op jit(solution)/shard_map/all_gather | solution.py:74
  85.0 0.0 collective-permute-done
  85.0 0.0 collective-permute-done.1
  85.1 0.3 maximum_convert_fusion
  85.4 0.2 slice.54
  85.6 1.0 fusion.5
  86.6 0.2 slice.57
  86.8 0.0 copy-start.2
  86.8 0.8 fusion.11
  87.6 0.0 collective-permute-done.3
  87.6 0.6 copy-done.2
  88.2 1.7 pad_maximum_fusion
  89.9 0.9 reverse_select_fusion
  90.8 1.2 fusion.15
  92.0 1.1 fusion.16
  93.2 0.0 all-reduce.4.cloned.1.call-update
  93.2 0.0 reduce-scatter.2.cloned.1.call-start
  93.2 72.2 %all-reduce.4.cloned.1.call-done = f32[192,256]{1,0:T(8,128)} async-done(((f32[192,256]{1,0:T(8,128)}), f32[192,256]{1,0:T(8,128)}) %all-reduce.4.cloned.1.call-update) | async-done | bytes 196624 | tf_op jit(solution)/shard_map/psum | solution.py:89
  165.5 1.0 add_convert_fusion
  166.4 0.0 copy-start.3
  166.4 1.8 fusion.17
  168.2 0.0 reduce-scatter.2.cloned.1.call-update
  168.2 0.0 copy-done.3
  168.2 30.3 %reduce-scatter.2.cloned.1.call-done = f32[512,256]{1,0:T(8,128)} async-done(((f32[2048,256]{1,0:T(8,128)}), f32[512,256]{1,0:T(8,128)}) %reduce-scatter.2.cloned.1.call-update) | async-done | bytes 524304 | tf_op jit(solution)/shard_map/reduce_scatter | solution.py:91
  198.6 1.9 broadcast_multiply_fusion
  (4 shorter events, 0.0 us)
Async XLA Ops:
  7.2 2.3 %copy-start = (bf16[64,4,2048]{2,1,0:T(4,128)(2,1)S(1)}, bf16[64,4,2048]{2,1,0:T(4,128)(2,1)}, u32[]{:S(2)}) copy-start(bf16[64,4,2048]{2,1,0:T(4,128)(2,1)} %param.7) | copy-start | bytes 3145732
  7.2 158.3 %all-reduce.4.cloned.1.call-start = ((), (), s32[]{:S(2)}) async-start(), calls=%async_computation.1 | async-start | bytes 393216 | tf_op jit(solution)/shard_map/psum | solution.py:89
  9.5 9.6 %copy-start.1 = (bf16[16,4,2048]{2,1,0:T(4,128)(2,1)S(1)}, bf16[16,4,2048]{2,1,0:T(4,128)(2,1)}, u32[]{:S(2)}) copy-start(bf16[16,4,2048]{2,1,0:T(4,128)(2,1)} %param.6) | copy-start | bytes 786436
  39.4 2.6 %collective-permute-start.2 = (bf16[1,192,2048]{2,1,0:T(8,128)(2,1)}, bf16[1,192,2048]{2,1,0:T(8,128)(2,1)S(1)}, u32[]{:S(2)}, u32[]{:S(2)}) collective-permute-start(bf16[1,192,2048]{2,1,0:T(8,128)(2,1)} %fusion.25), channel_id=1, source_target_pairs={{0,1},{1,0},{2,3},{3,2},{4,5},{5,4},{6,7},{7,6},{8,9},{9,8},{10,11... | collective-permute-start | bytes 2359304 | tf_op jit(solution)/shard_map/ppermute | solution.py:22
  44.3 8.3 %copy-start.4 = (bf16[192,256]{1,0:T(8,128)(2,1)S(1)}, bf16[192,256]{1,0:T(8,128)(2,1)}, u32[]{:S(2)}) copy-start(bf16[192,256]{1,0:T(8,128)(2,1)} %param.11) | copy-start | bytes 294916
  44.3 43.3 %collective-permute-start.3 = (bf16[2,192,2048]{2,1,0:T(8,128)(2,1)}, bf16[2,192,2048]{2,1,0:T(8,128)(2,1)}, u32[]{:S(2)}, u32[]{:S(2)}) collective-permute-start(bf16[2,192,2048]{2,1,0:T(8,128)(2,1)} %get-tuple-element.3), channel_id=1, source_target_pairs={{0,2},{1,3},{2,0},{3,1},{4,6},{5,7},{6,4},{7,5},{8,10},{9,11},{10,... | collective-permute-start | bytes 4718600 | tf_op jit(solution)/shard_map/ppermute | solution.py:22
  47.8 37.2 %collective-permute-start = (bf16[192,2,128]{0,2,1:T(8,128)(2,1)S(1)}, bf16[192,2,128]{0,2,1:T(8,128)(2,1)S(1)}, u32[]{:S(2)}, u32[]{:S(2)}) collective-permute-start(bf16[192,2,128]{0,2,1:T(8,128)(2,1)S(1)} %get-tuple-element.4), channel_id=1, source_target_pairs={{0,4},{4,8},{8,12},{12,16},{16,20},{20,24},{24,28},{1,5},{5,9},{9,... | collective-permute-start | bytes 294920 | tf_op jit(solution)/shard_map/ppermute | solution.py:39
  51.3 33.8 %collective-permute-start.1 = (bf16[192,2,128]{0,2,1:T(8,128)(2,1)S(1)}, bf16[192,2,128]{0,2,1:T(8,128)(2,1)S(1)}, u32[]{:S(2)}, u32[]{:S(2)}) collective-permute-start(bf16[192,2,128]{0,2,1:T(8,128)(2,1)S(1)} %get-tuple-element.5), channel_id=1, source_target_pairs={{4,0},{8,4},{12,8},{16,12},{20,16},{24,20},{28,24},{5,1},{9,5},{13... | collective-permute-start | bytes 294920 | tf_op jit(solution)/shard_map/ppermute | solution.py:40
  86.8 1.4 copy-start.2
  93.2 105.4 %reduce-scatter.2.cloned.1.call-start = ((), (), s32[]{:S(2)}) async-start(), calls=%async_computation.2 | async-start | bytes 2621440 | tf_op jit(solution)/shard_map/reduce_scatter | solution.py:91
  166.4 1.8 copy-start.3
Sparse Core Ops, SparseCore 0:
  93.3 72.1 all-reduce.3
  168.4 30.1 reduce-scatter.1
